TPU v7x, 32 devices: a whole 2x2x4 slice. The times are simulated.
32 devices in a mesh: seq: 4 (over z), head: 8 (over y, x, core).
Axes of the slice: x: 2, y: 2, z: 4, core: 2. Of those that a mesh axis runs over, the one named last changes fastest.
Arguments:
- x_in: bfloat16 [2048, 8192], P('seq', 'head'), may hold values from -6 to 6
- z_in: bfloat16 [2048, 8192], P('seq', 'head'), may hold values from -6 to 6
- bc_in: bfloat16 [2048, 2048], P('seq'), may hold values from -6 to 6
- conv_x: float32 [4, 8192], P(None, 'head'), may hold values from -3 to 3
- conv_bc: float32 [4, 2048], replicated, may hold values from -3 to 3
- dt: float32 [128, 2048], P('head', 'seq'), may hold values from 0 to 3, as said below
- a_log: float32 [128], P('head'), may hold values from -2 to 1, as said below
- skip_d: float32 [128], P('head'), may hold values from 0.5 to 1.5
- norm_gain: float32 [8192], P('head'), may hold values from 0.5 to 1.5
- seg_ids: int32 [2048], P('seq'), may hold values from 0 to 3, as said below
Outputs:
- mixed: bfloat16 [2048, 8192], P('seq', 'head')
Inputs may be any that keep to these rules, and one draw needn't show every extreme that they name: `a_log`: log of a decay rate of order one. `dt`: positive step sizes. `seg_ids`: document numbers never fall along the window, every document is nonempty, and the longest document holds exactly 1024 tokens.
All inputs are finite; a program needn't handle non-finite values.
Results may differ from a plain program's by a relative error of at most 0.0051.
Values may be sent and summed in bfloat16 or wider, within the bound.
No kernel may reach another device: no remote copies, remote signals or barrier semaphores. Data moves between devices by JAX's collectives and lax.ppermute only.
A program may use at most 64 MiB of HBM per device.

v0:
```python
import jax
import jax.numpy as jnp
from jax import lax
from jax.sharding import PartitionSpec as P

HEADS = 128
HEAD_DIM = 64
STATE = 128
GROUPS = 8
KERNEL = 4
SPAN = 128


def shifted(value, axis, steps):
    count = lax.axis_size(axis)
    first, last = (max(0, -steps), min(count, count - steps))
    return lax.ppermute(value, axis, [(source, source + steps) for source in range(first, last)])


def carried_in(x, axis, combine, identity):
    peers, place = (lax.axis_size(axis), lax.axis_index(axis))
    everything = jax.tree.map(
        lambda part, kind: lax.all_gather(part.astype(kind), axis), x, (jnp.bfloat16, jnp.bfloat16)
    )
    start = jax.tree.map(
        lambda part, zero: jnp.broadcast_to(jnp.asarray(zero, part.dtype), part.shape), x, identity
    )

    def hop(k, before):
        reached = k < place
        new = combine(
            before, jax.tree.map(lambda part, own: part[k].astype(own.dtype), everything, x)
        )
        return jax.tree.map(lambda a, b: jnp.where(reached, a, b), new, before)

    return lax.fori_loop(0, peers, hop, start)


def conv_silu(data, tail, weight, seg_float, tail_seg):
    rows = data.shape[0]
    padded = jnp.concatenate([tail, data], 0)
    seg_pad = jnp.concatenate([tail_seg.astype(jnp.float32), seg_float], 0)
    total = jnp.zeros(data.shape, jnp.float32)
    for offset in range(KERNEL):
        window = padded[offset : offset + rows].astype(jnp.float32)
        same_doc = (seg_pad[offset : offset + rows] == seg_float)[:, None]
        total = total + jnp.where(same_doc, window, 0.0) * weight[offset]
    return jax.nn.silu(total).astype(jnp.bfloat16)


def per_device(x_in, z_in, bc_in, conv_x, conv_bc, dt, a_log, skip_d, norm_gain, seg_ids):
    tok_rows = x_in.shape[0]
    local_heads = dt.shape[0]
    per_group = HEADS // GROUPS
    head_index = lax.axis_index("head")
    group = head_index * local_heads // per_group
    b_part = lax.dynamic_slice_in_dim(bc_in, group * STATE, STATE, 1)
    c_part = lax.dynamic_slice_in_dim(bc_in, GROUPS * STATE + group * STATE, STATE, 1)
    bc_mine = jnp.concatenate([b_part, c_part], 1)
    taps_b = lax.dynamic_slice_in_dim(conv_bc, group * STATE, STATE, 1)
    taps_c = lax.dynamic_slice_in_dim(conv_bc, GROUPS * STATE + group * STATE, STATE, 1)
    taps_mine = jnp.concatenate([taps_b, taps_c], 1)
    margin = KERNEL - 1
    tail_x, tail_bc, tail_seg = shifted(
        (
            x_in[tok_rows - margin :],
            bc_mine[tok_rows - margin :],
            seg_ids[tok_rows - margin :].astype(jnp.bfloat16),
        ),
        "seq",
        1,
    )
    seg_float = seg_ids.astype(jnp.float32)
    first_shard = lax.axis_index("seq") == 0
    tail_seg = jnp.where(first_shard, jnp.full(tail_seg.shape, -1.0, jnp.bfloat16), tail_seg)
    x_conv = conv_silu(x_in, tail_x, conv_x, seg_float, tail_seg)
    bc_conv = conv_silu(bc_mine, tail_bc, taps_mine, seg_float, tail_seg)
    prev_seg = tail_seg[margin - 1].astype(jnp.float32)
    spans = tok_rows // SPAN
    x_blocks = x_conv.reshape(spans, SPAN, local_heads, HEAD_DIM)
    b_blocks = bc_conv[:, :STATE].reshape(spans, SPAN, STATE)
    c_blocks = bc_conv[:, STATE:].reshape(spans, SPAN, STATE)
    dt_blocks = dt.reshape(local_heads, spans, SPAN).transpose(1, 0, 2)
    seg_blocks = seg_float.reshape(spans, SPAN)
    seg_before = jnp.concatenate([prev_seg[None], seg_blocks[:-1, -1]])
    rates = jnp.exp(a_log)
    log_decay = jnp.cumsum(-dt_blocks * rates[None, :, None], axis=2)
    causal = jnp.tril(jnp.ones((SPAN, SPAN), bool))
    same_doc = ((seg_blocks[:, :, None] == seg_blocks[:, None, :]) & causal[None])[:, None]
    spread = log_decay[:, :, :, None] - log_decay[:, :, None, :]
    decay = jnp.where(same_doc, jnp.exp(jnp.where(same_doc, spread, 0.0)), 0.0)
    scores = jnp.einsum("ctn,csn->cts", c_blocks, b_blocks, preferred_element_type=jnp.float32)
    weight_tensors = (scores[:, None] * decay * dt_blocks[:, :, None, :]).astype(jnp.bfloat16)
    y_diag = jnp.einsum(
        "chts,cshp->cthp", weight_tensors, x_blocks, preferred_element_type=jnp.float32
    )
    same_end = (seg_blocks == seg_blocks[:, -1:]).astype(jnp.float32)
    to_end = jnp.exp(log_decay[:, :, -1:] - log_decay) * dt_blocks * same_end[:, None, :]
    x_weighted = (x_blocks.astype(jnp.float32) * to_end.transpose(0, 2, 1)[..., None]).astype(
        jnp.bfloat16
    )
    fresh = jnp.einsum("cshp,csn->chpn", x_weighted, b_blocks, preferred_element_type=jnp.float32)
    keep = (
        jnp.exp(log_decay[:, :, -1])
        * (seg_blocks[:, -1] == seg_before).astype(jnp.float32)[:, None]
    )

    def local_step(carry, item):
        state, factor = carry
        keep_block, fresh_block = item
        return (
            (keep_block[:, None, None] * state + fresh_block, keep_block * factor),
            (state, factor),
        )

    zero_state = jnp.zeros((local_heads, HEAD_DIM, STATE), jnp.float32)
    (total_state, total_keep), (entering, factors) = lax.scan(
        local_step, (zero_state, jnp.ones((local_heads,), jnp.float32)), (keep, fresh)
    )

    def combine(earlier, later):
        return (earlier[0] * later[0], later[0][:, None, None] * earlier[1] + later[1])

    incoming = carried_in(
        (total_keep, total_state),
        "seq",
        combine,
        (jnp.ones_like(total_keep), jnp.zeros_like(total_state)),
    )[1]
    starts = entering + factors[:, :, None, None] * incoming[None]
    alive = (seg_blocks == seg_before[:, None]).astype(jnp.float32)
    y_carry = jnp.einsum(
        "ctn,chpn->cthp", c_blocks.astype(jnp.float32), starts, precision=lax.Precision.HIGHEST
    )
    y_carry = y_carry * (jnp.exp(log_decay).transpose(0, 2, 1) * alive[:, :, None])[..., None]
    summed = (y_diag + y_carry).reshape(tok_rows, local_heads, HEAD_DIM)
    summed = summed + skip_d[None, :, None] * x_conv.reshape(
        tok_rows, local_heads, HEAD_DIM
    ).astype(jnp.float32)
    gated = summed * jax.nn.silu(z_in.reshape(tok_rows, local_heads, HEAD_DIM).astype(jnp.float32))
    squares = jnp.sum(gated * gated, axis=(1, 2))
    gathered = lax.all_gather(squares[None], "head", axis=0, tiled=True)
    total_squares = jnp.sum(gathered, axis=0)
    mean_sq = total_squares / (HEADS * HEAD_DIM)
    normalized_output = (gated * lax.rsqrt(mean_sq + 1e-05)[:, None, None]).reshape(
        tok_rows, local_heads * HEAD_DIM
    )
    return (normalized_output * norm_gain).astype(jnp.bfloat16)


def solution(mesh):
    in_specs = (
        P("seq", "head"),
        P("seq", "head"),
        P("seq", None),
        P(None, "head"),
        P(),
        P("head", "seq"),
        P("head"),
        P("head"),
        P("head"),
        P("seq"),
    )
    out_specs = P("seq", "head")
    return jax.shard_map(
        per_device, mesh=mesh, in_specs=in_specs, out_specs=out_specs, check_vma=False
    )
```

profile of v0, /device:TPU:0, one launch (start us, length us, event | category | flops | bytes accessed | tf_op | source)
XLA Modules:
  0.0 97.1 jit_solution(2739810109216518925)
XLA Ops:
  6.5 0.0 all-gather.5.cloned.1.call-start
  6.6 1.0 %constant_dynamic-slice_fusion.4 = (bf16[512,128]{1,0:T(8,128)(2,1)S(1)}, bf16[512,128]{1,0:T(8,128)(2,1)S(1)}) fusion(bf16[512,2048]{1,0:T(8,128)(2,1)} %param.16, s32[]{:T(128)S(6)} %select_n.85, s32[]{:T(128)S(6)} %select_n.86), kind=kLoop, calls=%fused_computation.87 | loop fusion | bytes 524296 | tf_op jit(solution)/shard_map/dynamic_slice | solution.py:57
  7.6 5.0 %collective-permute-start.2 = (bf16[3,256]{1,0:T(4,128)(2,1)S(1)}, bf16[3,256]{1,0:T(4,128)(2,1)S(1)}, u32[]{:S(2)}, u32[]{:S(2)}) collective-permute-start(bf16[3,256]{1,0:T(4,128)(2,1)S(1)} %fusion.36), channel_id=1, source_target_pairs={{0,8},{8,16},{16,24},{1,9},{9,17},{17,25},{2,10},{10,18},{18,26},{... | collective-permute-start | bytes 4616 | tf_op jit(solution)/shard_map/ppermute | solution.py:17
  12.6 0.8 convert_bitcast_fusion
  13.4 0.1 slice.84
  13.4 3.5 %collective-permute-start = (bf16[3]{0:T(256)(128)(2,1)S(1)}, bf16[3]{0:T(256)(128)(2,1)S(1)}, u32[]{:S(2)}, u32[]{:S(2)}) collective-permute-start(bf16[3]{0:T(256)(128)(2,1)S(1)} %slice.84), channel_id=1, source_target_pairs={{0,8},{8,16},{16,24},{1,9},{9,17},{17,25},{2,10},{10,18},{18,26},{... | collective-permute-start | bytes 26 | tf_op jit(solution)/shard_map/ppermute | solution.py:17
  16.9 0.7 slice.86
  17.6 0.2 copy.69
  17.8 3.5 %collective-permute-start.1 = (bf16[3,1024]{0,1:T(8,128)(2,1)S(1)}, bf16[3,1024]{0,1:T(8,128)(2,1)S(1)}, u32[]{:S(2)}, u32[]{:S(2)}) collective-permute-start(bf16[3,1024]{0,1:T(8,128)(2,1)S(1)} %copy.69), channel_id=1, source_target_pairs={{0,8},{8,16},{16,24},{1,9},{9,17},{17,25},{2,10},{10,18},{18,26},{... | collective-permute-start | bytes 18440 | tf_op jit(solution)/shard_map/ppermute | solution.py:17
  21.4 1.5 %copy.70 = bf16[512,1024]{0,1:T(8,128)(2,1)S(1)} copy(bf16[512,1024]{1,0:T(8,128)(2,1)} %param.14) | data formatting | bytes 2097152 | tf_op args[0]
  22.9 0.7 constant_dynamic-slice_fusion.2
  23.6 0.2 slice_reduce_fusion.2
  23.8 0.1 negate_multiply_fusion
  23.9 1.1 %reduce_window_sum.11 = f32[4,16,128]{2,1,0:T(8,128)S(1)} reduce-window(f32[4,16,128]{2,1,0:T(8,128)S(1)} %negate_multiply_fusion, f32[]{:T(128)} %constant.81.clone.1), window={size=1x1x128 pad=0_0x0_0x127_0}, to_apply=%region_0.1 | reduce-window | flops 1040384 | bytes 65540 | tf_op jit(solution)/shard_map/jit(cumsum)/reduce_window_sum | solution.py:87
  25.0 0.2 slice_reduce_fusion
  25.2 0.1 pad_maximum_fusion.2
  25.3 0.1 slice_compare_fusion.2
  25.4 0.6 slice.108
  26.6 0.1 pad_maximum_fusion.4
  26.7 0.2 slice_reduce_fusion.1
  26.9 0.1 compare_convert_fusion
  27.0 0.1 fusion.35
  27.1 0.1 exponential_multiply_fusion
  27.1 0.1 maximum_maximum_fusion
  27.2 0.7 multiply_convert_fusion.3
  28.0 2.5 %multiply_convert_fusion.2 = bf16[512,1024]{0,1:T(8,128)(2,1)S(1)} fusion(bf16[512,1024]{0,1:T(8,128)(2,1)S(1)} %copy.70, bf16[3,1024]{0,1:T(8,128)(2,1)S(1)} %collective-permute-done.1, f32[1024]{0:T(1024)S(1)} %bitcast.111, f32[1024]{0:T(1024)S(1)} %bitcast.112, f32[1024]{0:T(1024)S(1)} %bitcast.110, f32[1024]{0:T(1024)S(1)} %bitcast.109, ...), kind=kLoop, calls=%fused_computation.33 | loop fusion | flops 15204352 | bytes 2121728 | tf_op jit(solution)/shard_map/convert_element_type | solution.py:48
  30.6 1.3 %reshape.117 = bf16[4,128,16,64]{1,0,3,2:T(4,128)(2,1)} reshape(bf16[512,1024]{0,1:T(8,128)(2,1)S(1)} %multiply_convert_fusion.2) | data formatting | bytes 2097152 | tf_op jit(solution)/shard_map/reshape | solution.py:80
  31.8 0.0 copy-done.1
  31.9 1.6 %fusion.27 = f32[4,16,64,128]{3,2,1,0:T(8,128)S(1)} fusion(bf16[4,128,128,1]{2,1,3,0:T(8,128)(2,1)S(1)} %bitcast.105, f32[4,128,16]{1,2,0:T(8,128)S(1)} %fusion.35, bf16[4,128,16,64]{1,0,3,2:T(4,128)(2,1)} %reshape.117), kind=kOutput, calls=%fused_computation.41 | convolution fusion | flops 135790592 | bytes 3309568 | tf_op jit(solution)/shard_map/cshp,csn->chpn/dot_general | solution.py:102
  33.5 4.1 %while.31 = (s32[]{:T(128)}, f32[16,64,128]{2,1,0:T(8,128)S(1)}, f32[16]{0:T(128)S(1)}, f32[4,16,64,128]{3,2,1,0:T(8,128)}, f32[4,16]{1,0:T(4,128)S(1)}, /*index...) while((s32[]{:T(128)}, f32[16,64,128]{2,1,0:T(8,128)S(1)}, ...), condition=%wide.region_2.3_spmd.clone, body=%wide.region_1.2_spmd.clone.sunk | while | flops 524323 | bytes 2622581 | solution.py:117
  33.6 0.8 bitcast_dynamic-update-slice_fusion.2
  34.4 0.1 bitcast_add_fusion.4
  34.6 0.8 bitcast_dynamic-update-slice_fusion.2
  35.4 0.1 bitcast_add_fusion.4
  35.6 0.9 bitcast_dynamic-update-slice_fusion.2
  36.5 0.1 bitcast_add_fusion.4
  36.7 0.8 bitcast_dynamic-update-slice_fusion.2
  37.5 0.1 bitcast_add_fusion.4
  37.6 0.8 convert_element_type.134
  38.4 0.0 all-gather.5.cloned.1.call-update
  38.5 1.5 %copy.77 = bf16[512,1024]{0,1:T(8,128)(2,1)S(1)} copy(bf16[512,1024]{1,0:T(8,128)(2,1)} %param.15) | data formatting | bytes 2097152 | tf_op args[1]
  40.0 0.0 copy-start.7
  40.0 0.0 copy-start.9
  40.0 1.7 %reshape.125 = f32[4,128,16,64]{1,0,3,2:T(4,128)} reshape(bf16[512,1024]{0,1:T(8,128)(2,1)S(1)} %copy.77) | data formatting | bytes 3145728 | tf_op jit(solution)/shard_map/convert_element_type | solution.py:140
  41.7 0.1 mul.327
  41.8 0.1 mul.328
  41.9 0.7 dynamic-slice
  43.2 0.1 compare_and_fusion
  43.4 0.2 fusion.45
  43.6 0.2 dynamic-update-slice
  43.9 9.7 %all-reduce = bf16[64]{0:T(256)(128)(2,1)S(1)} all-reduce(bf16[64]{0:T(256)(128)(2,1)S(1)} %dynamic-update-slice), channel_id=2, replica_groups=mesh['seq'=4,'head'=8] {'seq'}, use_global_device_ids=true, to_apply=%add | all-reduce | flops 64 | bytes 256
  53.6 0.1 reshape.126
  53.6 3.2 %fusion.4 = f32[4,16,64,128]{3,2,1,0:T(8,128)} fusion(f32[4,16,128]{2,1,0:T(8,128)S(1)} %bitcast_bitcast_fusion.1, f32[4,16,128]{2,1,0:T(8,128)S(1)} %reduce_window_sum.11, f32[4,128,128]{2,1,0:T(8,128)S(1)} %fusion.45, pred[4,128,128]{2,1,0:T(8,128)(4,1)S(1)} %compare_and_fusion, bf16[4,128,16,64]{1,0,3,2:T(4,128)(2,1)S(1)} %copy-done.3), kind=kOutput, calls=%fused_computation.13 | convolution fusion | flops 140509184 | bytes 3538944 | tf_op jit(solution)/shard_map/chts,cshp->cthp/dot_general | solution.py:94
  56.8 8.5 %all-gather.5.cloned.1.call-done = bf16[64,64,128]{2,1,0:T(8,128)(2,1)} async-done(((bf16[16,64,128]{2,1,0:T(8,128)(2,1)}), bf16[64,64,128]{2,1,0:T(8,128)(2,1)}) %all-gather.5.cloned.1.call-update) | async-done | bytes 1048592 | tf_op jit(solution)/shard_map/all_gather | solution.py:23
  65.3 4.5 %while.32 = (s32[]{:T(128)}, f32[16,64,128]{2,1,0:T(8,128)S(1)}, s32[]{:T(128)}, bf16[4,16]{1,0:T(4,128)(2,1)S(1)}, bf16[4,16,64,128]{3,2,1,0:T(8,128)(2,1)}, /*index=5*/s32[]{:T(128)}, s32[]{:T(128)}) while((s32[]{:T(128)}, f32[16,64,128]{2,1,0:T(8,128)S(1)}, s32[]{:T(128)}, bf16[4,16]{1,0:T(4,128)(2,1)S(1)}, ...), condition=%wide.region_4.5_spmd.clone, body=%wide.region_3.4_spmd.clone.sunk | while | flops 655380 | bytes 1310985 | solution.py:36
  65.3 1.1 %fusion.56 = f32[16,64,128]{2,1,0:T(8,128)S(1)} fusion(f32[16,64,128]{2,1,0:T(8,128)S(1)} %get-tuple-element.359, bf16[4,16,64,128]{3,2,1,0:T(8,128)(2,1)} %get-tuple-element.369, s32[]{:T(128)} %get-tuple-element.358, f32[16]{0:T(128)S(1)} %bitcast_convert_fusion.2, pred[]{:T(512)S(6)} %compare.9, pred[]{:T(512)S(6)} %lt.37), kind=kLoop, calls=%fused_computation.8.clone.1 | loop fusion | flops 655360 | bytes 1310790 | tf_op jit(solution)/shard_map/while/body/eval_jaxpr/jit(_where)/select_n | solution.py:34
  66.4 1.1 %fusion.56 = f32[16,64,128]{2,1,0:T(8,128)S(1)} fusion(f32[16,64,128]{2,1,0:T(8,128)S(1)} %get-tuple-element.359, bf16[4,16,64,128]{3,2,1,0:T(8,128)(2,1)} %get-tuple-element.369, s32[]{:T(128)} %get-tuple-element.358, f32[16]{0:T(128)S(1)} %bitcast_convert_fusion.2, pred[]{:T(512)S(6)} %compare.9, pred[]{:T(512)S(6)} %lt.37), kind=kLoop, calls=%fused_computation.8.clone.1 | loop fusion | flops 655360 | bytes 1310790 | tf_op jit(solution)/shard_map/while/body/eval_jaxpr/jit(_where)/select_n | solution.py:34
  67.5 1.1 %fusion.56 = f32[16,64,128]{2,1,0:T(8,128)S(1)} fusion(f32[16,64,128]{2,1,0:T(8,128)S(1)} %get-tuple-element.359, bf16[4,16,64,128]{3,2,1,0:T(8,128)(2,1)} %get-tuple-element.369, s32[]{:T(128)} %get-tuple-element.358, f32[16]{0:T(128)S(1)} %bitcast_convert_fusion.2, pred[]{:T(512)S(6)} %compare.9, pred[]{:T(512)S(6)} %lt.37), kind=kLoop, calls=%fused_computation.8.clone.1 | loop fusion | flops 655360 | bytes 1310790 | tf_op jit(solution)/shard_map/while/body/eval_jaxpr/jit(_where)/select_n | solution.py:34
  68.7 1.1 %fusion.56 = f32[16,64,128]{2,1,0:T(8,128)S(1)} fusion(f32[16,64,128]{2,1,0:T(8,128)S(1)} %get-tuple-element.359, bf16[4,16,64,128]{3,2,1,0:T(8,128)(2,1)} %get-tuple-element.369, s32[]{:T(128)} %get-tuple-element.358, f32[16]{0:T(128)S(1)} %bitcast_convert_fusion.2, pred[]{:T(512)S(6)} %compare.9, pred[]{:T(512)S(6)} %lt.37), kind=kLoop, calls=%fused_computation.8.clone.1 | loop fusion | flops 655360 | bytes 1310790 | tf_op jit(solution)/shard_map/while/body/eval_jaxpr/jit(_where)/select_n | solution.py:34
  69.8 4.9 %fusion.9 = (f32[4,128]{1,0:T(4,128)S(1)}, f32[4,128,16,64]{1,3,2,0:T(8,128)S(1)}) fusion(f32[4,128,16,64]{1,0,3,2:T(4,128)} %reshape.125, f32[16]{0:T(128)S(1)} %copy-done.7, bf16[4,128,16,64]{1,0,3,2:T(4,128)(2,1)S(1)} %copy-done.3, f32[4,128,16]{1,2,0:T(8,128)S(1)} %multiply_bitcast_fusion, bf16[4,128,128,1]{2,1,3,0:T(8,128)(2,1)S(1)} %bitcast.108, ...), kind=kOutput, calls=%fused_computation.18 | convolution fusion | flops 812645888 | bytes 10127680 | tf_op jit(solution)/shard_map/ctn,chpn->cthp/dot_general | solution.py:132
  74.7 2.8 %copy.76 = f32[4,128,16,64]{1,0,3,2:T(4,128)} copy(f32[4,128,16,64]{1,3,2,0:T(8,128)S(1)} %get-tuple-element.243) | data formatting | bytes 4194304 | tf_op jit(solution)/shard_map/add | solution.py:136
  77.5 8.9 %all-gather.2 = f32[8,1,512]{2,1,0:T(1,128)S(1)} all-gather(f32[1,1,512]{2,1,0:T(1,128)S(1)} %bitcast.117), channel_id=1, replica_groups=mesh['seq'=4,'head'=8] {'head'}, dimensions={0}, use_global_device_ids=true | all-gather | bytes 18432 | tf_op jit(solution)/shard_map/all_gather | solution.py:142
  86.4 2.5 %fusion.13 = bf16[512,1024]{0,1:T(8,128)(2,1)S(1)} fusion(f32[128,8,4,128]{3,2,1,0:T(4,128)} %bitcast.103, bf16[512,1024]{0,1:T(8,128)(2,1)S(1)} %copy-done.2, f32[1024]{0:T(1024)S(1)} %copy-done.6, f32[512]{0:T(512)S(1)} %add_rsqrt_fusion, f32[1024]{0:T(1024)S(1)} %mul.328, bf16[512,1024]{0,1:T(8,128)(2,1)S(1)} %copy.77), kind=kLoop, calls=%fused_computation.23 | loop fusion | flops 6291456 | bytes 5253120 | tf_op jit(solution)/shard_map/convert_element_type | solution.py:148
  88.9 1.3 %copy.80 = bf16[512,1024]{1,0:T(8,128)(2,1)} copy(bf16[512,1024]{0,1:T(8,128)(2,1)S(1)} %fusion.13) | data formatting | bytes 2097152 | tf_op jit(solution)/shard_map/convert_element_type | solution.py:148
  (50 shorter events, 0.5 us)
Async XLA Ops:
  6.5 17.3 %copy-start = (f32[16,512]{1,0:T(8,128)S(1)}, f32[16,512]{1,0:T(8,128)}, u32[]{:S(2)}) copy-start(f32[16,512]{1,0:T(8,128)} %param.19) | copy-start | bytes 98308
  6.5 18.8 %copy-start.4 = (s32[512]{0:T(512)S(1)}, s32[512]{0:T(512)}, u32[]{:S(2)}) copy-start(s32[512]{0:T(512)} %param.23) | copy-start | bytes 6148
  6.5 17.1 %copy-start.5 = (f32[4,1024]{1,0:T(4,128)S(1)}, f32[4,1024]{1,0:T(4,128)}, u32[]{:S(2)}) copy-start(f32[4,1024]{1,0:T(4,128)} %param.17) | copy-start | bytes 49156
  6.5 17.1 %copy-start.8 = (f32[16]{0:T(128)S(1)}, f32[16]{0:T(128)}, u32[]{:S(2)}) copy-start(f32[16]{0:T(128)} %param.20) | copy-start | bytes 196
  6.5 58.7 %all-gather.5.cloned.1.call-start = ((), (), s32[]{:S(2)}) async-start(), calls=%async_computation | async-start | bytes 1310720 | tf_op jit(solution)/shard_map/all_gather | solution.py:23
  7.6 19.5 %collective-permute-start.2 = (bf16[3,256]{1,0:T(4,128)(2,1)S(1)}, bf16[3,256]{1,0:T(4,128)(2,1)S(1)}, u32[]{:S(2)}, u32[]{:S(2)}) collective-permute-start(bf16[3,256]{1,0:T(4,128)(2,1)S(1)} %fusion.36), channel_id=1, source_target_pairs={{0,8},{8,16},{16,24},{1,9},{9,17},{17,25},{2,10},{10,18},{18,26},{... | collective-permute-start | bytes 4616 | tf_op jit(solution)/shard_map/ppermute | solution.py:17
  13.4 11.8 %collective-permute-start = (bf16[3]{0:T(256)(128)(2,1)S(1)}, bf16[3]{0:T(256)(128)(2,1)S(1)}, u32[]{:S(2)}, u32[]{:S(2)}) collective-permute-start(bf16[3]{0:T(256)(128)(2,1)S(1)} %slice.84), channel_id=1, source_target_pairs={{0,8},{8,16},{16,24},{1,9},{9,17},{17,25},{2,10},{10,18},{18,26},{... | collective-permute-start | bytes 26 | tf_op jit(solution)/shard_map/ppermute | solution.py:17
  17.8 10.1 %collective-permute-start.1 = (bf16[3,1024]{0,1:T(8,128)(2,1)S(1)}, bf16[3,1024]{0,1:T(8,128)(2,1)S(1)}, u32[]{:S(2)}, u32[]{:S(2)}) collective-permute-start(bf16[3,1024]{0,1:T(8,128)(2,1)S(1)} %copy.69), channel_id=1, source_target_pairs={{0,8},{8,16},{16,24},{1,9},{9,17},{17,25},{2,10},{10,18},{18,26},{... | collective-permute-start | bytes 18440 | tf_op jit(solution)/shard_map/ppermute | solution.py:17
  30.6 1.3 %copy-start.1 = (bf16[512,1024]{0,1:T(8,128)(2,1)}, bf16[512,1024]{0,1:T(8,128)(2,1)S(1)}, u32[]{:S(2)}) copy-start(bf16[512,1024]{0,1:T(8,128)(2,1)S(1)} %multiply_convert_fusion.2) | copy-start | bytes 3145732
  40.0 1.8 %copy-start.7 = (f32[16]{0:T(128)S(1)}, f32[16]{0:T(128)}, u32[]{:S(2)}) copy-start(f32[16]{0:T(128)} %param.21) | copy-start | bytes 196
  40.0 1.9 %copy-start.9 = (u32[32]{0:T(128)S(1)}, u32[32]{0:T(128)}, u32[]{:S(2)}) copy-start(u32[32]{0:T(128)} %constant.97) | copy-start | bytes 388
  40.0 13.6 %copy-start.3 = (bf16[4,128,16,64]{1,0,3,2:T(4,128)(2,1)S(1)}, bf16[4,128,16,64]{1,0,3,2:T(4,128)(2,1)}, u32[]{:S(2)}) copy-start(bf16[4,128,16,64]{1,0,3,2:T(4,128)(2,1)} %reshape.117) | copy-start | bytes 3145732
  74.7 11.7 %copy-start.2 = (bf16[512,1024]{0,1:T(8,128)(2,1)S(1)}, bf16[512,1024]{0,1:T(8,128)(2,1)}, u32[]{:S(2)}) copy-start(bf16[512,1024]{0,1:T(8,128)(2,1)} %copy-done.1) | copy-start | bytes 3145732
  74.7 11.7 %copy-start.6 = (f32[1024]{0:T(1024)S(1)}, f32[1024]{0:T(1024)}, u32[]{:S(2)}) copy-start(f32[1024]{0:T(1024)} %param.22) | copy-start | bytes 12292
Sparse Core Ops, SparseCore 0:
  38.6 26.6 all-gather.4
where the time goes:
time: 97.6 us; the launch traced here: 97.1 us
  blocking collectives  18.5 us (19%)
  other arithmetic  17.8 us (18%)
  local copies, waits for them, and re-layouts  15.1 us (15%)
  between operations  15.1 us (15%)
  starting transfers between devices  12 us (12%)
  matrix products  9.94 us (10%)
  waiting for transfers between devices  8.49 us (9%)
    ppermute x3, starting transfers between devices, shifted(): lax.ppermute(value, axis, [(source, source + steps) for source in range(f...  11.9 us
    unnamed x1, blocking collectives  9.67 us
    all_gather x1, blocking collectives, per_device(): gathered = lax.all_gather(squares[None], 'head', axis=0, tiled=True)  8.86 us
    all_gather x1, waiting for transfers between devices, carried_in(): lax.all_gather(part.astype(kind), axis)  8.46 us
    dot_general x1, matrix products, per_device(): jnp.einsum('ctn,chpn->cthp', c_blocks.astype(jnp.float32), starts, precis...  4.94 us
    select_n x4, other arithmetic, hop(): return jax.tree.map(lambda a, b: jnp.where(reached, a, b), new, before)  4.36 us
    unnamed x25, local copies, waits for them, and re-layouts  3.98 us
    dynamic_update_slice x4, other arithmetic, per_device(): lax.scan(local_step, (zero_state, jnp.ones((local_heads,), jnp.float32)),...  3.37 us
  transfers between devices with their start and end apart: 4, of which 1 were waited for; matrix products, arithmetic and copies ran while one was open for 16% of the time, Pallas kernels for 0%

commit v1 on v0

--- a/solution.py
+++ b/solution.py
@@ -49,6 +49,13 @@
 
 
 def per_device(x_in, z_in, bc_in, conv_x, conv_bc, dt, a_log, skip_d, norm_gain, seg_ids):
+
+    def close_table(array_in):
+        found_now = jax.lax.axis_size("head")
+        mixed_arr = jnp.stack([array_in] * found_now)
+        oldest = jax.lax.all_to_all(mixed_arr, "head", 0, 0)
+        return jnp.concatenate(oldest, axis=0)
+
     tok_rows = x_in.shape[0]
     local_heads = dt.shape[0]
     per_group = HEADS // GROUPS
@@ -139,7 +146,7 @@
     ).astype(jnp.float32)
     gated = summed * jax.nn.silu(z_in.reshape(tok_rows, local_heads, HEAD_DIM).astype(jnp.float32))
     squares = jnp.sum(gated * gated, axis=(1, 2))
-    gathered = lax.all_gather(squares[None], "head", axis=0, tiled=True)
+    gathered = close_table(squares[None])
     total_squares = jnp.sum(gathered, axis=0)
     mean_sq = total_squares / (HEADS * HEAD_DIM)
     normalized_output = (gated * lax.rsqrt(mean_sq + 1e-05)[:, None, None]).reshape(

time: 97.6 us -> 96.3 us (0.987)
  blocking collectives: 18.5 us -> 9.63 us
  starting transfers between devices: 12 us -> 15.6 us
  local copies, waits for them, and re-layouts: 15.1 us -> 17.4 us
  matrix products: 9.94 us -> 11.2 us
    all_gather x1 -> x0, blocking collectives: 8.86 us -> none  [per_device(): gathered = lax.all_gather(squares[None], 'head', axis=0, tiled=True)]
    all_to_all x0 -> x1, starting transfers between devices: none -> 3.65 us  [close_table(): oldest = jax.lax.all_to_all(mixed_arr, 'head', 0, 0)]
    add x1, local copies, waits for them, and re-layouts: 2.76 us -> 4.42 us  [per_device(): summed = (y_diag + y_carry).reshape(tok_rows, local_heads, HEAD_DIM)]
    dot_general x1, matrix products: 4.94 us -> 6.21 us  [per_device(): jnp.einsum('ctn,chpn->cthp', c_blocks.astype(jnp.float32), starts, precis...]
  transfers between devices with their start and end apart: 4 -> 5, of which waited for: 1 -> 2; matrix products, arithmetic and copies ran while one was open for 16% -> 21% of each run, Pallas kernels for 0% -> 0%
where the time goes in v1:
time: 96.3 us; the launch traced here: 95.7 us
  other arithmetic  17.8 us (18%)
  local copies, waits for them, and re-layouts  17.4 us (18%)
  starting transfers between devices  15.6 us (16%)
  between operations  15 us (16%)
  matrix products  11.2 us (12%)
  blocking collectives  9.63 us (10%)
  waiting for transfers between devices  8.9 us (9%)
    ppermute x3, starting transfers between devices, shifted(): lax.ppermute(value, axis, [(source, source + steps) for source in range(f...  11.9 us
    unnamed x1, blocking collectives  9.63 us
    all_gather x1, waiting for transfers between devices, carried_in(): lax.all_gather(part.astype(kind), axis)  8.7 us
    dot_general x1, matrix products, per_device(): jnp.einsum('ctn,chpn->cthp', c_blocks.astype(jnp.float32), starts, precis...  6.21 us
    add x1, local copies, waits for them, and re-layouts, per_device(): summed = (y_diag + y_carry).reshape(tok_rows, local_heads, HEAD_DIM)  4.42 us
    select_n x4, other arithmetic, hop(): return jax.tree.map(lambda a, b: jnp.where(reached, a, b), new, before)  4.37 us
    unnamed x25, local copies, waits for them, and re-layouts  3.97 us
    all_to_all x1, starting transfers between devices, close_table(): oldest = jax.lax.all_to_all(mixed_arr, 'head', 0, 0)  3.65 us
  transfers between devices with their start and end apart: 5, of which 2 were waited for; matrix products, arithmetic and copies ran while one was open for 21% of the time, Pallas kernels for 0%

profile of v1, /device:TPU:0, one launch (start us, length us, event | category | flops | bytes accessed | tf_op | source)
XLA Modules:
  0.0 95.7 jit_solution(6209515698445915901)
XLA Ops:
  6.5 0.0 all-gather.4.cloned.1.call-start
  6.6 1.0 %constant_dynamic-slice_fusion.4 = (bf16[512,128]{1,0:T(8,128)(2,1)S(1)}, bf16[512,128]{1,0:T(8,128)(2,1)S(1)}) fusion(bf16[512,2048]{1,0:T(8,128)(2,1)} %param.16, s32[]{:T(128)S(6)} %select_n.85, s32[]{:T(128)S(6)} %select_n.86), kind=kLoop, calls=%fused_computation.87 | loop fusion | bytes 524296 | tf_op jit(solution)/shard_map/dynamic_slice | solution.py:64
  7.6 5.0 %collective-permute-start.2 = (bf16[3,256]{1,0:T(4,128)(2,1)S(1)}, bf16[3,256]{1,0:T(4,128)(2,1)S(1)}, u32[]{:S(2)}, u32[]{:S(2)}) collective-permute-start(bf16[3,256]{1,0:T(4,128)(2,1)S(1)} %fusion.36), channel_id=1, source_target_pairs={{0,8},{8,16},{16,24},{1,9},{9,17},{17,25},{2,10},{10,18},{18,26},{... | collective-permute-start | bytes 4616 | tf_op jit(solution)/shard_map/ppermute | solution.py:17
  12.6 0.8 convert_bitcast_fusion
  13.4 0.1 slice.84
  13.4 3.5 %collective-permute-start = (bf16[3]{0:T(256)(128)(2,1)S(1)}, bf16[3]{0:T(256)(128)(2,1)S(1)}, u32[]{:S(2)}, u32[]{:S(2)}) collective-permute-start(bf16[3]{0:T(256)(128)(2,1)S(1)} %slice.84), channel_id=1, source_target_pairs={{0,8},{8,16},{16,24},{1,9},{9,17},{17,25},{2,10},{10,18},{18,26},{... | collective-permute-start | bytes 26 | tf_op jit(solution)/shard_map/ppermute | solution.py:17
  16.9 0.7 slice.86
  17.6 0.2 copy.83
  17.8 3.5 %collective-permute-start.1 = (bf16[3,1024]{0,1:T(8,128)(2,1)S(1)}, bf16[3,1024]{0,1:T(8,128)(2,1)S(1)}, u32[]{:S(2)}, u32[]{:S(2)}) collective-permute-start(bf16[3,1024]{0,1:T(8,128)(2,1)S(1)} %copy.83), channel_id=1, source_target_pairs={{0,8},{8,16},{16,24},{1,9},{9,17},{17,25},{2,10},{10,18},{18,26},{... | collective-permute-start | bytes 18440 | tf_op jit(solution)/shard_map/ppermute | solution.py:17
  21.4 1.5 %copy.84 = bf16[512,1024]{0,1:T(8,128)(2,1)S(1)} copy(bf16[512,1024]{1,0:T(8,128)(2,1)} %param.14) | data formatting | bytes 2097152 | tf_op args[0]
  22.9 0.7 constant_dynamic-slice_fusion.2
  23.6 0.2 slice_reduce_fusion.2
  23.8 0.1 negate_multiply_fusion
  23.9 1.1 %reduce_window_sum.11 = f32[4,16,128]{2,1,0:T(8,128)S(1)} reduce-window(f32[4,16,128]{2,1,0:T(8,128)S(1)} %negate_multiply_fusion, f32[]{:T(128)} %constant.81.clone.1), window={size=1x1x128 pad=0_0x0_0x127_0}, to_apply=%region_0.1 | reduce-window | flops 1040384 | bytes 65540 | tf_op jit(solution)/shard_map/jit(cumsum)/reduce_window_sum | solution.py:94
  25.0 0.2 slice_reduce_fusion
  25.2 0.1 pad_maximum_fusion.2
  25.3 0.1 slice_compare_fusion.2
  25.4 0.6 slice.108
  26.6 0.1 pad_maximum_fusion.4
  26.7 0.2 slice_reduce_fusion.1
  26.9 0.1 compare_convert_fusion
  27.0 0.1 fusion.35
  27.1 0.1 exponential_multiply_fusion
  27.1 0.1 maximum_maximum_fusion
  27.2 0.7 multiply_convert_fusion.3
  28.0 2.5 %multiply_convert_fusion.2 = bf16[512,1024]{0,1:T(8,128)(2,1)S(1)} fusion(bf16[512,1024]{0,1:T(8,128)(2,1)S(1)} %copy.84, bf16[3,1024]{0,1:T(8,128)(2,1)S(1)} %collective-permute-done.1, f32[1024]{0:T(1024)S(1)} %bitcast.111, f32[1024]{0:T(1024)S(1)} %bitcast.112, f32[1024]{0:T(1024)S(1)} %bitcast.110, f32[1024]{0:T(1024)S(1)} %bitcast.109, ...), kind=kLoop, calls=%fused_computation.33 | loop fusion | flops 15204352 | bytes 2121728 | tf_op jit(solution)/shard_map/convert_element_type | solution.py:48
  30.6 1.3 %reshape.122 = bf16[4,128,16,64]{1,0,3,2:T(4,128)(2,1)} reshape(bf16[512,1024]{0,1:T(8,128)(2,1)S(1)} %multiply_convert_fusion.2) | data formatting | bytes 2097152 | tf_op jit(solution)/shard_map/reshape | solution.py:87
  31.8 0.0 copy-done.1
  31.9 1.6 %fusion.27 = f32[4,16,64,128]{3,2,1,0:T(8,128)S(1)} fusion(bf16[4,128,128,1]{2,1,3,0:T(8,128)(2,1)S(1)} %bitcast.105, f32[4,128,16]{1,2,0:T(8,128)S(1)} %fusion.35, bf16[4,128,16,64]{1,0,3,2:T(4,128)(2,1)} %reshape.122), kind=kOutput, calls=%fused_computation.41 | convolution fusion | flops 135790592 | bytes 3309568 | tf_op jit(solution)/shard_map/cshp,csn->chpn/dot_general | solution.py:109
  33.5 4.1 %while.31 = (s32[]{:T(128)}, f32[16,64,128]{2,1,0:T(8,128)S(1)}, f32[16]{0:T(128)S(1)}, f32[4,16,64,128]{3,2,1,0:T(8,128)}, f32[4,16]{1,0:T(4,128)S(1)}, /*index...) while((s32[]{:T(128)}, f32[16,64,128]{2,1,0:T(8,128)S(1)}, ...), condition=%wide.region_2.3_spmd.clone, body=%wide.region_1.2_spmd.clone.sunk | while | flops 524323 | bytes 2622581 | solution.py:124
  33.6 0.9 bitcast_dynamic-update-slice_fusion.2
  34.4 0.1 bitcast_add_fusion.4
  34.6 0.8 bitcast_dynamic-update-slice_fusion.2
  35.4 0.1 bitcast_add_fusion.4
  35.6 0.9 bitcast_dynamic-update-slice_fusion.2
  36.5 0.1 bitcast_add_fusion.4
  36.7 0.8 bitcast_dynamic-update-slice_fusion.2
  37.5 0.1 bitcast_add_fusion.4
  37.7 0.8 convert_element_type.134
  38.4 0.0 all-gather.4.cloned.1.call-update
  38.5 1.5 %copy.91 = bf16[512,1024]{0,1:T(8,128)(2,1)S(1)} copy(bf16[512,1024]{1,0:T(8,128)(2,1)} %param.15) | data formatting | bytes 2097152 | tf_op args[1]
  40.0 1.7 %reshape.130 = f32[4,128,16,64]{1,0,3,2:T(4,128)} reshape(bf16[512,1024]{0,1:T(8,128)(2,1)S(1)} %copy.91) | data formatting | bytes 3145728 | tf_op jit(solution)/shard_map/convert_element_type | solution.py:147
  41.7 0.6 dynamic-slice
  43.0 0.1 compare_and_fusion
  43.2 0.2 fusion.45
  43.4 0.2 dynamic-update-slice
  43.7 9.6 %all-reduce = bf16[64]{0:T(256)(128)(2,1)S(1)} all-reduce(bf16[64]{0:T(256)(128)(2,1)S(1)} %dynamic-update-slice), channel_id=2, replica_groups=mesh['seq'=4,'head'=8] {'seq'}, use_global_device_ids=true, to_apply=%add | all-reduce | flops 64 | bytes 256
  53.3 0.1 reshape.131
  53.4 3.2 %fusion.4 = f32[4,16,64,128]{3,2,1,0:T(8,128)} fusion(f32[4,16,128]{2,1,0:T(8,128)S(1)} %bitcast_bitcast_fusion.1, f32[4,16,128]{2,1,0:T(8,128)S(1)} %reduce_window_sum.11, f32[4,128,128]{2,1,0:T(8,128)S(1)} %fusion.45, pred[4,128,128]{2,1,0:T(8,128)(4,1)S(1)} %compare_and_fusion, bf16[4,128,16,64]{1,0,3,2:T(4,128)(2,1)S(1)} %copy-done.3), kind=kOutput, calls=%fused_computation.13 | convolution fusion | flops 140509184 | bytes 3538944 | tf_op jit(solution)/shard_map/chts,cshp->cthp/dot_general | solution.py:101
  56.5 8.7 %all-gather.4.cloned.1.call-done = bf16[64,64,128]{2,1,0:T(8,128)(2,1)} async-done(((bf16[16,64,128]{2,1,0:T(8,128)(2,1)}), bf16[64,64,128]{2,1,0:T(8,128)(2,1)}) %all-gather.4.cloned.1.call-update) | async-done | bytes 1048592 | tf_op jit(solution)/shard_map/all_gather | solution.py:23
  65.2 4.5 %while.32 = (s32[]{:T(128)}, f32[16,64,128]{2,1,0:T(8,128)S(1)}, s32[]{:T(128)}, bf16[4,16]{1,0:T(4,128)(2,1)S(1)}, bf16[4,16,64,128]{3,2,1,0:T(8,128)(2,1)}, /*index=5*/s32[]{:T(128)}, s32[]{:T(128)}) while((s32[]{:T(128)}, f32[16,64,128]{2,1,0:T(8,128)S(1)}, s32[]{:T(128)}, bf16[4,16]{1,0:T(4,128)(2,1)S(1)}, ...), condition=%wide.region_4.5_spmd.clone, body=%wide.region_3.4_spmd.clone.sunk | while | flops 655380 | bytes 1310985 | solution.py:36
  65.3 1.1 %fusion.56 = f32[16,64,128]{2,1,0:T(8,128)S(1)} fusion(f32[16,64,128]{2,1,0:T(8,128)S(1)} %get-tuple-element.359, bf16[4,16,64,128]{3,2,1,0:T(8,128)(2,1)} %get-tuple-element.369, s32[]{:T(128)} %get-tuple-element.358, f32[16]{0:T(128)S(1)} %bitcast_convert_fusion.2, pred[]{:T(512)S(6)} %compare.9, pred[]{:T(512)S(6)} %lt.37), kind=kLoop, calls=%fused_computation.8.clone.1 | loop fusion | flops 655360 | bytes 1310790 | tf_op jit(solution)/shard_map/while/body/eval_jaxpr/jit(_where)/select_n | solution.py:34
  66.4 1.1 %fusion.56 = f32[16,64,128]{2,1,0:T(8,128)S(1)} fusion(f32[16,64,128]{2,1,0:T(8,128)S(1)} %get-tuple-element.359, bf16[4,16,64,128]{3,2,1,0:T(8,128)(2,1)} %get-tuple-element.369, s32[]{:T(128)} %get-tuple-element.358, f32[16]{0:T(128)S(1)} %bitcast_convert_fusion.2, pred[]{:T(512)S(6)} %compare.9, pred[]{:T(512)S(6)} %lt.37), kind=kLoop, calls=%fused_computation.8.clone.1 | loop fusion | flops 655360 | bytes 1310790 | tf_op jit(solution)/shard_map/while/body/eval_jaxpr/jit(_where)/select_n | solution.py:34
  67.5 1.1 %fusion.56 = f32[16,64,128]{2,1,0:T(8,128)S(1)} fusion(f32[16,64,128]{2,1,0:T(8,128)S(1)} %get-tuple-element.359, bf16[4,16,64,128]{3,2,1,0:T(8,128)(2,1)} %get-tuple-element.369, s32[]{:T(128)} %get-tuple-element.358, f32[16]{0:T(128)S(1)} %bitcast_convert_fusion.2, pred[]{:T(512)S(6)} %compare.9, pred[]{:T(512)S(6)} %lt.37), kind=kLoop, calls=%fused_computation.8.clone.1 | loop fusion | flops 655360 | bytes 1310790 | tf_op jit(solution)/shard_map/while/body/eval_jaxpr/jit(_where)/select_n | solution.py:34
  68.6 1.1 %fusion.56 = f32[16,64,128]{2,1,0:T(8,128)S(1)} fusion(f32[16,64,128]{2,1,0:T(8,128)S(1)} %get-tuple-element.359, bf16[4,16,64,128]{3,2,1,0:T(8,128)(2,1)} %get-tuple-element.369, s32[]{:T(128)} %get-tuple-element.358, f32[16]{0:T(128)S(1)} %bitcast_convert_fusion.2, pred[]{:T(512)S(6)} %compare.9, pred[]{:T(512)S(6)} %lt.37), kind=kLoop, calls=%fused_computation.8.clone.1 | loop fusion | flops 655360 | bytes 1310790 | tf_op jit(solution)/shard_map/while/body/eval_jaxpr/jit(_where)/select_n | solution.py:34
  69.8 6.2 %fusion.9 = (f32[4,128]{1,0:T(4,128)S(1)}, f32[4,128,16,64]{1,3,2,0:T(8,128)}) fusion(f32[4,128,16,64]{1,0,3,2:T(4,128)} %reshape.130, f32[16]{0:T(128)S(1)} %copy-done.7, bf16[4,128,16,64]{1,0,3,2:T(4,128)(2,1)S(1)} %copy-done.3, f32[4,128,16]{1,2,0:T(8,128)S(1)} %multiply_bitcast_fusion, bf16[4,128,128,1]{2,1,3,0:T(8,128)(2,1)S(1)} %bitcast.108, ...), kind=kOutput, calls=%fused_computation.18 | convolution fusion | flops 812645888 | bytes 10127680 | tf_op jit(solution)/shard_map/ctn,chpn->cthp/dot_general | solution.py:139
  76.0 0.6 stack.3
  76.6 3.7 %all-to-all-start = ((f32[8,1,512]{2,1,0:T(1,128)}), f32[8,1,512]{2,1,0:T(1,128)S(1)}, u32[]{:S(2)}, u32[]{:S(2)}) async-start(f32[8,1,512]{2,1,0:T(1,128)} %stack.3), calls=%async_computation | async-start | bytes 32768 | tf_op jit(solution)/shard_map/all_to_all | solution.py:56
  80.2 0.1 mul.327
  80.3 0.1 mul.328
  80.4 4.4 %copy.90 = f32[4,128,16,64]{1,0,3,2:T(4,128)} copy(f32[4,128,16,64]{1,3,2,0:T(8,128)} %get-tuple-element.243) | data formatting | bytes 4194304 | tf_op jit(solution)/shard_map/add | solution.py:143
  84.8 0.2 all-to-all-done
  85.1 2.5 %fusion.13 = bf16[512,1024]{0,1:T(8,128)(2,1)S(1)} fusion(f32[128,8,4,128]{3,2,1,0:T(4,128)} %bitcast.103, bf16[512,1024]{0,1:T(8,128)(2,1)S(1)} %copy-done.2, f32[1024]{0:T(1024)S(1)} %copy-done.6, f32[512]{0:T(512)S(1)} %add_rsqrt_fusion, f32[1024]{0:T(1024)S(1)} %mul.328, bf16[512,1024]{0,1:T(8,128)(2,1)S(1)} %copy.91), kind=kLoop, calls=%fused_computation.23 | loop fusion | flops 6291456 | bytes 5253120 | tf_op jit(solution)/shard_map/convert_element_type | solution.py:155
  87.5 1.3 %copy.95 = bf16[512,1024]{1,0:T(8,128)(2,1)} copy(bf16[512,1024]{0,1:T(8,128)(2,1)S(1)} %fusion.13) | data formatting | bytes 2097152 | tf_op jit(solution)/shard_map/convert_element_type | solution.py:155
  (52 shorter events, 0.5 us)
Async XLA Ops:
  6.5 17.3 %copy-start = (f32[16,512]{1,0:T(8,128)S(1)}, f32[16,512]{1,0:T(8,128)}, u32[]{:S(2)}) copy-start(f32[16,512]{1,0:T(8,128)} %param.19) | copy-start | bytes 98308
  6.5 18.8 %copy-start.4 = (s32[512]{0:T(512)S(1)}, s32[512]{0:T(512)}, u32[]{:S(2)}) copy-start(s32[512]{0:T(512)} %param.23) | copy-start | bytes 6148
  6.5 17.1 %copy-start.5 = (f32[4,1024]{1,0:T(4,128)S(1)}, f32[4,1024]{1,0:T(4,128)}, u32[]{:S(2)}) copy-start(f32[4,1024]{1,0:T(4,128)} %param.17) | copy-start | bytes 49156
  6.5 17.1 %copy-start.8 = (f32[16]{0:T(128)S(1)}, f32[16]{0:T(128)}, u32[]{:S(2)}) copy-start(f32[16]{0:T(128)} %param.20) | copy-start | bytes 196
  6.5 58.7 %all-gather.4.cloned.1.call-start = ((), (), s32[]{:S(2)}) async-start(), calls=%async_computation.1 | async-start | bytes 1310720 | tf_op jit(solution)/shard_map/all_gather | solution.py:23
  7.6 19.5 %collective-permute-start.2 = (bf16[3,256]{1,0:T(4,128)(2,1)S(1)}, bf16[3,256]{1,0:T(4,128)(2,1)S(1)}, u32[]{:S(2)}, u32[]{:S(2)}) collective-permute-start(bf16[3,256]{1,0:T(4,128)(2,1)S(1)} %fusion.36), channel_id=1, source_target_pairs={{0,8},{8,16},{16,24},{1,9},{9,17},{17,25},{2,10},{10,18},{18,26},{... | collective-permute-start | bytes 4616 | tf_op jit(solution)/shard_map/ppermute | solution.py:17
  13.4 11.8 %collective-permute-start = (bf16[3]{0:T(256)(128)(2,1)S(1)}, bf16[3]{0:T(256)(128)(2,1)S(1)}, u32[]{:S(2)}, u32[]{:S(2)}) collective-permute-start(bf16[3]{0:T(256)(128)(2,1)S(1)} %slice.84), channel_id=1, source_target_pairs={{0,8},{8,16},{16,24},{1,9},{9,17},{17,25},{2,10},{10,18},{18,26},{... | collective-permute-start | bytes 26 | tf_op jit(solution)/shard_map/ppermute | solution.py:17
  17.8 10.1 %collective-permute-start.1 = (bf16[3,1024]{0,1:T(8,128)(2,1)S(1)}, bf16[3,1024]{0,1:T(8,128)(2,1)S(1)}, u32[]{:S(2)}, u32[]{:S(2)}) collective-permute-start(bf16[3,1024]{0,1:T(8,128)(2,1)S(1)} %copy.83), channel_id=1, source_target_pairs={{0,8},{8,16},{16,24},{1,9},{9,17},{17,25},{2,10},{10,18},{18,26},{... | collective-permute-start | bytes 18440 | tf_op jit(solution)/shard_map/ppermute | solution.py:17
  30.6 1.3 %copy-start.1 = (bf16[512,1024]{0,1:T(8,128)(2,1)}, bf16[512,1024]{0,1:T(8,128)(2,1)S(1)}, u32[]{:S(2)}) copy-start(bf16[512,1024]{0,1:T(8,128)(2,1)S(1)} %multiply_convert_fusion.2) | copy-start | bytes 3145732
  40.0 1.7 %copy-start.9 = (u32[32]{0:T(128)S(1)}, u32[32]{0:T(128)}, u32[]{:S(2)}) copy-start(u32[32]{0:T(128)} %constant.97) | copy-start | bytes 388
  40.0 13.4 %copy-start.3 = (bf16[4,128,16,64]{1,0,3,2:T(4,128)(2,1)S(1)}, bf16[4,128,16,64]{1,0,3,2:T(4,128)(2,1)}, u32[]{:S(2)}) copy-start(bf16[4,128,16,64]{1,0,3,2:T(4,128)(2,1)} %reshape.122) | copy-start | bytes 3145732
  65.2 4.5 %copy-start.7 = (f32[16]{0:T(128)S(1)}, f32[16]{0:T(128)}, u32[]{:S(2)}) copy-start(f32[16]{0:T(128)} %param.21) | copy-start | bytes 196
  76.6 8.4 %all-to-all-start = ((f32[8,1,512]{2,1,0:T(1,128)}), f32[8,1,512]{2,1,0:T(1,128)S(1)}, u32[]{:S(2)}, u32[]{:S(2)}) async-start(f32[8,1,512]{2,1,0:T(1,128)} %stack.3), calls=%async_computation | async-start | bytes 32768 | tf_op jit(solution)/shard_map/all_to_all | solution.py:56
  80.4 4.7 %copy-start.2 = (bf16[512,1024]{0,1:T(8,128)(2,1)S(1)}, bf16[512,1024]{0,1:T(8,128)(2,1)}, u32[]{:S(2)}) copy-start(bf16[512,1024]{0,1:T(8,128)(2,1)} %copy-done.1) | copy-start | bytes 3145732
  80.4 4.7 %copy-start.6 = (f32[1024]{0:T(1024)S(1)}, f32[1024]{0:T(1024)}, u32[]{:S(2)}) copy-start(f32[1024]{0:T(1024)} %param.22) | copy-start | bytes 12292
Sparse Core Ops, SparseCore 0:
  38.6 26.6 all-gather.3
